TPU v7x, 32 devices: a whole 2x2x4 slice. The times are simulated.
32 devices in a mesh: feed: 4 (over y, core), tm: 8 (over z, x).
Axes of the slice: x: 2, y: 2, z: 4, core: 2. Of those that a mesh axis runs over, the one named last changes fastest.
Arguments:
- tod: bfloat16 [8192, 50, 256], P(('feed', 'tm')), may hold values from -6 to 6
- pixels: int32 [8192, 50], P(('feed', 'tm')), may hold values from 0 to 31
- block_slots: int32 [8192], P(('feed', 'tm')), may hold values from 0 to 7, as said below
- tile_lists: int32 [32, 8, 1], P(('feed', 'tm')), may hold values from -1 to 63, as said below
- tile_place: int32 [64], replicated, may hold values from 0 to 63, as said below
- prior: float32 [256], replicated, may hold values from 0.5 to 4
Outputs:
- drift_levels: float32 [8192, 256], P(('feed', 'tm'))
- leftover_error: float32 [8192, 256], P(('feed', 'tm'))
- destriped_result_map: float32 [64, 32, 256], P('tm', None, 'feed')
Inputs may be any that keep to these rules, and one draw needn't show every extreme that they name: tile_lists[g, o, s] is -1 or a tile whose tile_place // 8 equals o; the live entries of one device are distinct; entries 0 and 7 of each device's flattened list are live; some tiles are named by no list. block_slots[b] names a live entry of the flattened list of the device that holds baseline b. tile_place is a permutation of the tiles; place p is stored by tm index p // 8 in its row p % 8.
All inputs are finite; a program needn't handle non-finite values.
Results may differ from a plain program's by a relative error of at most 0.0013.
Values sent between devices are 32-bit elements; how exact they have to be, the bound alone decides.
No kernel may reach another device: no remote copies, remote signals or barrier semaphores. Data moves between devices by JAX's collectives and lax.ppermute only.
A program may use at most 64 MiB of HBM per device.

v0:
```python
import jax
import jax.numpy as jnp
from jax import lax
from jax.sharding import PartitionSpec as P

CELLS_IN_PATCH = 32
ITERS = 2


def local(tod, pixels, block_slots, tile_lists, tile_place, prior):
    highest = lax.Precision.HIGHEST
    tm_count = lax.axis_size("tm")
    feed_count = lax.axis_size("feed")
    slot_count = tile_lists.shape[1] * tile_lists.shape[2]
    tile_total = tile_place.shape[0]
    rows_owned = tile_total // tm_count
    owner_index = lax.axis_index("tm")
    block_count = tod.shape[0]
    sample_count = tod.shape[1]
    channels = tod.shape[2]
    share_width = channels // feed_count
    pix_match = pixels[:, :, None] == jnp.arange(CELLS_IN_PATCH, dtype=jnp.int32)[None, None, :]
    hit_blocks = jnp.sum(pix_match.astype(jnp.float32), axis=1)
    slot_hot = (block_slots[:, None] == jnp.arange(slot_count, dtype=jnp.int32)[None, :]).astype(
        jnp.float32
    )
    weights = (slot_hot[:, :, None] * hit_blocks[:, None, :]).reshape(
        block_count, slot_count * CELLS_IN_PATCH
    )
    hit_slots = jnp.sum(weights, axis=0).reshape(slot_count, CELLS_IN_PATCH)
    my_list = tile_lists.reshape(slot_count)
    recv_hits, recv_tiles = (
        lax.all_to_all(hit_slots, "tm", split_axis=0, concat_axis=0, tiled=True),
        lax.all_to_all(my_list, "tm", split_axis=0, concat_axis=0, tiled=True),
    )
    matches = recv_tiles[:, None] == jnp.arange(tile_total, dtype=jnp.int32)[None, :]
    recv_place = jnp.sum(jnp.where(matches, tile_place[None, :] + 1, 0), axis=1) - 1
    local_rows = owner_index * rows_owned + jnp.arange(rows_owned, dtype=jnp.int32)
    select = (local_rows[:, None] == recv_place[None, :]).astype(jnp.float32)
    owned_hits = jnp.dot(select, recv_hits, precision=highest)
    hits = lax.psum(owned_hits, "feed")
    inverse = 1.0 / jnp.maximum(hits, 1.0)

    def averaged_patch_lines(slot_parts):
        received = lax.all_to_all(slot_parts, "tm", split_axis=0, concat_axis=0, tiled=True)
        owned_sum = jnp.einsum("lk,kpc->lpc", select, received, precision=highest)
        summed = lax.psum(owned_sum, "feed")
        return summed * inverse[:, :, None]

    def project(slot_parts, sample_sums):
        sky_tiles = averaged_patch_lines(slot_parts)
        outgoing = jnp.einsum("lk,lpc->kpc", select, sky_tiles, precision=highest)
        returned = lax.all_to_all(outgoing, "tm", split_axis=0, concat_axis=0, tiled=True)
        flat_tiles = returned.reshape(slot_count * CELLS_IN_PATCH, channels)
        mapped = jnp.dot(weights, flat_tiles, precision=highest)
        return sample_sums - mapped

    def unrolled_drift_levels(values):
        parts_flat = jnp.einsum("bq,bc->qc", weights, values, precision=highest)
        return parts_flat.reshape(slot_count, CELLS_IN_PATCH, channels)

    def squares(values):
        return lax.psum(jnp.sum(values * values), ("feed", "tm"))

    pix_hot = pix_match.astype(jnp.bfloat16)
    per_block = jnp.einsum("bsp,bsc->bpc", pix_hot, tod, preferred_element_type=jnp.float32)
    observation_segments = jnp.einsum("bk,bpc->kpc", slot_hot, per_block, precision=highest)
    data_sums = jnp.sum(per_block, axis=1)
    system_target = project(observation_segments, data_sums)
    drift_levels = jnp.zeros_like(system_target)
    leftover_error = system_target
    descent_direction = system_target
    norm_now = squares(leftover_error)
    for number in range(ITERS):
        image = (
            project(unrolled_drift_levels(descent_direction), sample_count * descent_direction)
            + prior[None, :] * descent_direction
        )
        update_factor = norm_now / lax.psum(jnp.sum(descent_direction * image), ("feed", "tm"))
        drift_levels = drift_levels + update_factor * descent_direction
        leftover_error = leftover_error - update_factor * image
        norm_next = squares(leftover_error)
        descent_direction = leftover_error + norm_next / norm_now * descent_direction
        norm_now = norm_next
    converged_patch_lines = averaged_patch_lines(
        observation_segments - unrolled_drift_levels(drift_levels)
    )
    destriped_result_map = lax.dynamic_slice_in_dim(
        converged_patch_lines, lax.axis_index("feed") * share_width, share_width, 2
    )
    return (drift_levels, leftover_error, destriped_result_map)


def solution(mesh):
    return jax.shard_map(
        local,
        mesh=mesh,
        in_specs=(
            P(("feed", "tm"), None, None),
            P(("feed", "tm"), None),
            P(("feed", "tm")),
            P(("feed", "tm"), None, None),
            P(),
            P(),
        ),
        out_specs=(P(("feed", "tm"), None), P(("feed", "tm"), None), P("tm", None, "feed")),
        check_vma=False,
    )
```

profile of v0, /device:TPU:0, one launch (start us, length us, event | category | flops | bytes accessed | tf_op | source)
XLA Modules:
  0.0 404.3 jit_solution(7255400728901228236)
XLA Ops:
  7.2 1.3 copy.88
  8.5 7.3 %all-to-all-start = ((s32[8,1,1]{2,1,0:T(1,128)}), s32[8,1,1]{2,1,0:T(1,128)S(1)}, u32[]{:S(2)}, u32[]{:S(2)}) async-start(s32[8,1,1]{2,1,0:T(1,128)} %copy.88), calls=%async_computation | async-start | bytes 8192 | tf_op jit(solution)/shard_map/all_to_all | solution.py:34
  15.8 0.9 copy.85
  16.7 1.2 convert_reduce_fusion
  17.8 0.0 copy-start.1
  17.9 7.7 %fusion.54 = (f32[256,256]{1,0:T(8,128)S(1)}, f32[256,32,256]{2,1,0:T(8,128)S(1)}) fusion(bf16[256,50,256]{2,0,1:T(8,128)(2,1)} %param.6, s32[256,50]{1,0:T(8,128)S(1)} %copy.85), kind=kOutput, calls=%fused_computation.78 | convolution fusion | flops 212156416 | bytes 15255552 | tf_op jit(solution)/shard_map/bsp,bsc->bpc/dot_general | solution.py:66
  25.6 0.0 copy-start.3
  25.6 0.0 copy-start.2
  25.6 7.7 %fusion = f32[8,32,256]{2,0,1:T(8,128)S(1)} fusion(f32[256,32,256]{2,1,0:T(8,128)S(1)} %get-tuple-element.30, s32[256]{0:T(256)S(1)} %copy-done.1), kind=kOutput, calls=%fused_computation | convolution fusion | flops 201328640 | bytes 8651776 | tf_op jit(solution)/shard_map/bk,bpc->kpc/dot_general | solution.py:67
  33.3 0.1 copy.87
  33.4 0.7 multiply_bitcast_fusion
  34.1 0.0 all-to-all-done
  34.1 6.0 %all-to-all-start.2 = ((f32[8,1,32]{2,1,0:T(1,128)}), f32[8,1,32]{2,1,0:T(1,128)S(1)}, u32[]{:S(2)}, u32[]{:S(2)}) async-start(f32[8,1,32]{2,1,0:T(1,128)} %bitcast.4), calls=%async_computation.2 | async-start | bytes 8192 | tf_op jit(solution)/shard_map/all_to_all | solution.py:33
  40.1 0.8 copy.90
  40.9 0.2 reduce.1
  41.1 5.4 %all-to-all-done.2 = f32[8,1,32]{2,1,0:T(1,128)S(1)} async-done(((f32[8,1,32]{2,1,0:T(1,128)}), f32[8,1,32]{2,1,0:T(1,128)S(1)}, u32[]{:S(2)}, u32[]{:S(2)}) %all-to-all-start.2) | async-done | bytes 1056 | tf_op jit(solution)/shard_map/all_to_all | solution.py:33
  46.5 3.4 all-to-all-start.1
  49.9 0.0 all-reduce.6.cloned.1.call-start
  50.0 0.2 select_reduce_fusion
  50.2 0.2 fusion.49
  50.4 5.9 %psum.64 = f32[8,32]{1,0:T(8,128)S(1)} all-reduce(f32[8,32]{1,0:T(8,128)S(1)} %fusion.49), channel_id=1, replica_groups=mesh['feed'=4,'tm'=8] {'feed'}, use_global_device_ids=true, to_apply=%region_5.6 | all-reduce | flops 256 | bytes 2048 | tf_op jit(solution)/shard_map/psum | solution.py:41
  56.3 1.8 all-to-all-done.1
  58.1 1.1 fusion.25
  59.2 0.0 all-reduce.6.cloned.1.call-update
  59.2 0.0 all-reduce.8.cloned.1.call-start
  59.3 0.1 copy.92
  59.4 31.9 %all-reduce.6.cloned.1.call-done = f32[8,32,256]{2,0,1:T(8,128)} async-done(((f32[8,32,256]{2,0,1:T(8,128)}), f32[8,32,256]{2,0,1:T(8,128)}) %all-reduce.6.cloned.1.call-update) | async-done | bytes 262160 | tf_op jit(solution)/shard_map/psum | solution.py:47
  91.2 1.3 fusion.31
  92.6 0.1 copy.94
  92.7 13.5 %all_to_all.56 = f32[8,32,256]{2,1,0:T(8,128)S(1)} all-to-all(f32[8,32,256]{2,1,0:T(8,128)S(1)} %copy.94), channel_id=1, replica_groups=mesh['feed'=4,'tm'=8] {'tm'}, dimensions={0} | all-to-all | bytes 524288 | tf_op jit(solution)/shard_map/all_to_all | solution.py:53
  106.2 0.6 fusion.5
  106.8 0.4 fusion.16
  107.2 11.1 %all_to_all.57 = f32[8,32,256]{2,1,0:T(8,128)S(1)} all-to-all(f32[8,32,256]{2,1,0:T(8,128)S(1)} %fusion.16), channel_id=1, replica_groups=mesh['feed'=4,'tm'=8] {'tm'}, dimensions={0} | all-to-all | bytes 524288 | tf_op jit(solution)/shard_map/all_to_all | solution.py:45
  118.3 1.1 fusion.23
  119.5 0.0 all-reduce.8.cloned.1.call-update
  119.5 0.0 all-reduce.10.cloned.1.call-start
  119.5 31.2 %all-reduce.8.cloned.1.call-done = f32[8,32,256]{2,0,1:T(8,128)} async-done(((f32[8,32,256]{2,0,1:T(8,128)}), f32[8,32,256]{2,0,1:T(8,128)}) %all-reduce.8.cloned.1.call-update) | async-done | bytes 262160 | tf_op jit(solution)/shard_map/psum | solution.py:47
  150.8 1.3 fusion.29
  152.1 0.1 copy.97
  152.2 13.5 %all_to_all.58 = f32[8,32,256]{2,1,0:T(8,128)S(1)} all-to-all(f32[8,32,256]{2,1,0:T(8,128)S(1)} %copy.97), channel_id=1, replica_groups=mesh['feed'=4,'tm'=8] {'tm'}, dimensions={0} | all-to-all | bytes 524288 | tf_op jit(solution)/shard_map/all_to_all | solution.py:53
  165.7 1.2 multiply_reduce_fusion.3
  167.0 38.0 %all-reduce = (f32[]{:T(128)}, f32[]{:T(128)}) all-reduce(f32[]{:T(128)} %get-tuple-element.22, f32[]{:T(128)} %get-tuple-element.21), channel_id=1, replica_groups=mesh['feed'=4,'tm'=8] {'feed','tm'}, use_global_device_ids=true, to_apply=%region_7.8 | all-reduce | flops 2 | bytes 16 | tf_op jit(solution)/shard_map/psum | solution.py:63
  206.3 0.7 multiply_reduce_fusion.2
  207.0 41.4 %psum.68 = f32[]{:T(128)} all-reduce(f32[]{:T(128)} %multiply_reduce_fusion.2), channel_id=1, replica_groups=mesh['feed'=4,'tm'=8] {'feed','tm'}, use_global_device_ids=true, to_apply=%region_12.13 | all-reduce | flops 1 | bytes 8 | tf_op jit(solution)/shard_map/psum | solution.py:63
  249.8 0.4 fusion.14
  250.2 12.5 %all_to_all.59 = f32[8,32,256]{2,1,0:T(8,128)S(1)} all-to-all(f32[8,32,256]{2,1,0:T(8,128)S(1)} %fusion.14), channel_id=1, replica_groups=mesh['feed'=4,'tm'=8] {'tm'}, dimensions={0} | all-to-all | bytes 524288 | tf_op jit(solution)/shard_map/all_to_all | solution.py:45
  262.7 1.1 fusion.21
  263.8 0.0 all-reduce.10.cloned.1.call-update
  263.8 0.0 all-reduce.12.cloned.1.call-start
  263.9 30.5 %all-reduce.10.cloned.1.call-done = f32[8,32,256]{2,0,1:T(8,128)} async-done(((f32[8,32,256]{2,0,1:T(8,128)}), f32[8,32,256]{2,0,1:T(8,128)}) %all-reduce.10.cloned.1.call-update) | async-done | bytes 262160 | tf_op jit(solution)/shard_map/psum | solution.py:47
  294.4 1.3 fusion.27
  295.8 0.1 copy.100
  295.9 13.5 %all_to_all.60 = f32[8,32,256]{2,1,0:T(8,128)S(1)} all-to-all(f32[8,32,256]{2,1,0:T(8,128)S(1)} %copy.100), channel_id=1, replica_groups=mesh['feed'=4,'tm'=8] {'tm'}, dimensions={0} | all-to-all | bytes 524288 | tf_op jit(solution)/shard_map/all_to_all | solution.py:53
  309.4 1.2 multiply_reduce_fusion.1
  310.6 37.9 %psum.70 = f32[]{:T(128)} all-reduce(f32[]{:T(128)} %get-tuple-element.32), channel_id=1, replica_groups=mesh['feed'=4,'tm'=8] {'feed','tm'}, use_global_device_ids=true, to_apply=%region_15.16 | all-reduce | flops 1 | bytes 8 | tf_op jit(solution)/shard_map/psum | solution.py:79
  349.9 0.8 multiply_subtract_fusion
  350.7 0.5 convolution_subtract_fusion
  351.2 0.1 copy.102
  351.3 13.1 %all_to_all.61 = f32[8,32,256]{2,1,0:T(8,128)S(1)} all-to-all(f32[8,32,256]{2,1,0:T(8,128)S(1)} %copy.102), channel_id=1, replica_groups=mesh['feed'=4,'tm'=8] {'tm'}, dimensions={0} | all-to-all | bytes 524288 | tf_op jit(solution)/shard_map/all_to_all | solution.py:45
  364.3 1.1 fusion.18
  365.5 0.0 all-reduce.12.cloned.1.call-update
  365.5 30.6 %all-reduce.12.cloned.1.call-done = f32[8,32,256]{2,0,1:T(8,128)} async-done(((f32[8,32,256]{2,0,1:T(8,128)}), f32[8,32,256]{2,0,1:T(8,128)}) %all-reduce.12.cloned.1.call-update) | async-done | bytes 262160 | tf_op jit(solution)/shard_map/psum | solution.py:47
  396.1 1.0 dynamic-slice_multiply_fusion
  397.1 0.7 copy.104
  (10 shorter events, 0.1 us)
Async XLA Ops:
  8.5 25.6 %all-to-all-start = ((s32[8,1,1]{2,1,0:T(1,128)}), s32[8,1,1]{2,1,0:T(1,128)S(1)}, u32[]{:S(2)}, u32[]{:S(2)}) async-start(s32[8,1,1]{2,1,0:T(1,128)} %copy.88), calls=%async_computation | async-start | bytes 8192 | tf_op jit(solution)/shard_map/all_to_all | solution.py:34
  17.8 7.8 %copy-start.1 = (s32[256]{0:T(256)S(1)}, s32[256]{0:T(256)}, u32[]{:S(2)}) copy-start(s32[256]{0:T(256)} %param.8) | copy-start | bytes 3076
  25.6 14.5 %copy-start.3 = (s32[64]{0:T(128)S(1)}, s32[64]{0:T(128)}, u32[]{:S(2)}) copy-start(s32[64]{0:T(128)} %param.10) | copy-start | bytes 772
  25.6 140.1 %copy-start.2 = (f32[256]{0:T(256)S(1)}, f32[256]{0:T(256)}, u32[]{:S(2)}) copy-start(f32[256]{0:T(256)} %param.11) | copy-start | bytes 3076
  34.1 12.4 %all-to-all-start.2 = ((f32[8,1,32]{2,1,0:T(1,128)}), f32[8,1,32]{2,1,0:T(1,128)S(1)}, u32[]{:S(2)}, u32[]{:S(2)}) async-start(f32[8,1,32]{2,1,0:T(1,128)} %bitcast.4), calls=%async_computation.2 | async-start | bytes 8192 | tf_op jit(solution)/shard_map/all_to_all | solution.py:33
  46.5 11.6 %all-to-all-start.1 = ((f32[8,32,256]{2,1,0:T(8,128)}), f32[8,32,256]{2,1,0:T(8,128)S(1)}, u32[]{:S(2)}, u32[]{:S(2)}) async-start(f32[8,32,256]{2,1,0:T(8,128)} %copy.90), calls=%async_computation.1 | async-start | bytes 524288 | tf_op jit(solution)/shard_map/all_to_all | solution.py:45
  49.9 41.3 %all-reduce.6.cloned.1.call-start = ((), (), s32[]{:S(2)}) async-start(), calls=%async_computation.9 | async-start | bytes 524288 | tf_op jit(solution)/shard_map/psum | solution.py:47
  59.2 91.5 %all-reduce.8.cloned.1.call-start = ((), (), s32[]{:S(2)}) async-start(), calls=%async_computation.10 | async-start | bytes 524288 | tf_op jit(solution)/shard_map/psum | solution.py:47
  119.5 174.9 %all-reduce.10.cloned.1.call-start = ((), (), s32[]{:S(2)}) async-start(), calls=%async_computation.11 | async-start | bytes 524288 | tf_op jit(solution)/shard_map/psum | solution.py:47
  263.8 132.2 %all-reduce.12.cloned.1.call-start = ((), (), s32[]{:S(2)}) async-start(), calls=%async_computation.12 | async-start | bytes 524288 | tf_op jit(solution)/shard_map/psum | solution.py:47
  350.7 47.1 %copy-start = (f32[256,256]{1,0:T(8,128)}, f32[256,256]{1,0:T(8,128)S(1)}, u32[]{:S(2)}) copy-start(f32[256,256]{1,0:T(8,128)S(1)} %get-tuple-element.26) | copy-start | bytes 786436
Sparse Core Ops, SparseCore 0:
  59.4 31.8 all-reduce.5
  119.6 31.1 all-reduce.7
  264.0 30.4 all-reduce.9
  365.6 30.4 all-reduce.11
where the time goes:
time: 405 us; the launch traced here: 404 us
  blocking collectives  201 us (50%)
  waiting for transfers between devices  131 us (32%)
  matrix products  28.3 us (7%)
  between operations  18 us (4%)
  starting transfers between devices  16.9 us (4%)
  other arithmetic  4.82 us (1%)
  local copies, waits for them, and re-layouts  4.22 us (1%)
    psum x4, waiting for transfers between devices, averaged_patch_lines(): summed = lax.psum(owned_sum, 'feed')  124 us
    psum x2, blocking collectives, squares(): return lax.psum(jnp.sum(values * values), ('feed', 'tm'))  79.4 us
    all_to_all x3, blocking collectives, project(): lax.all_to_all(outgoing, 'tm', split_axis=0, concat_axis=0, tiled=True)  40.6 us
    psum x1, blocking collectives, local(): lax.psum(jnp.sum(descent_direction * image), ('feed', 'tm'))  37.9 us
    all_to_all x3, blocking collectives, averaged_patch_lines(): lax.all_to_all(slot_parts, 'tm', split_axis=0, concat_axis=0, tiled=True)  36.8 us
  transfers between devices with their start and end apart: 7, of which 6 were waited for; matrix products, arithmetic and copies ran while one was open for 5% of the time, Pallas kernels for 0%

commit v1 on v0

--- a/solution.py
+++ b/solution.py
@@ -44,7 +44,7 @@
     def averaged_patch_lines(slot_parts):
         received = lax.all_to_all(slot_parts, "tm", split_axis=0, concat_axis=0, tiled=True)
         owned_sum = jnp.einsum("lk,kpc->lpc", select, received, precision=highest)
-        summed = lax.psum(owned_sum, "feed")
+        summed = jnp.sum(lax.all_gather(owned_sum, "feed"), axis=0)
         return summed * inverse[:, :, None]
 
     def project(slot_parts, sample_sums):

time: 405 us -> 338 us (0.83)
  waiting for transfers between devices: 131 us -> 52.9 us
  blocking collectives: 201 us -> 214 us
    psum x4 -> x0, waiting for transfers between devices: 124 us -> none  [averaged_patch_lines(): summed = lax.psum(owned_sum, 'feed')]
    all_gather x0 -> x4, waiting for transfers between devices: none -> 44.8 us  [averaged_patch_lines(): summed = jnp.sum(lax.all_gather(owned_sum, 'feed'), axis=0)]
    all_to_all x0 -> x1, blocking collectives: none -> 9.73 us  [local(): lax.all_to_all(hit_slots, 'tm', split_axis=0, concat_axis=0, tiled=True)]
    all_to_all x1, waiting for transfers between devices: 1.8 us -> 8.01 us  [averaged_patch_lines(): lax.all_to_all(slot_parts, 'tm', split_axis=0, concat_axis=0, tiled=True)]
    all_to_all x1 -> x0, starting transfers between devices: 6 us -> none  [local(): lax.all_to_all(hit_slots, 'tm', split_axis=0, concat_axis=0, tiled=True)]
    all_to_all x1 -> x0, waiting for transfers between devices: 5.38 us -> none  [local(): lax.all_to_all(hit_slots, 'tm', split_axis=0, concat_axis=0, tiled=True)]
    reduce_sum x0 -> x4, other arithmetic: none -> 5.29 us  [averaged_patch_lines(): summed = jnp.sum(lax.all_gather(owned_sum, 'feed'), axis=0)]
  transfers between devices with their start and end apart: 7 -> 6, of which waited for: 6 -> 4; matrix products, arithmetic and copies ran while one was open for 5% -> 6% of each run, Pallas kernels for 0% -> 0%
where the time goes in v1:
time: 338 us; the launch traced here: 337 us
  blocking collectives  214 us (63%)
  waiting for transfers between devices  52.9 us (16%)
  matrix products  25.5 us (8%)
  between operations  18 us (5%)
  starting transfers between devices  13.4 us (4%)
  other arithmetic  8.63 us (3%)
  local copies, waits for them, and re-layouts  4.22 us (1%)
    psum x2, blocking collectives, squares(): return lax.psum(jnp.sum(values * values), ('feed', 'tm'))  79.7 us
    all_gather x4, waiting for transfers between devices, averaged_patch_lines(): summed = jnp.sum(lax.all_gather(owned_sum, 'feed'), axis=0)  44.8 us
    all_to_all x3, blocking collectives, project(): lax.all_to_all(outgoing, 'tm', split_axis=0, concat_axis=0, tiled=True)  42.7 us
    psum x1, blocking collectives, local(): lax.psum(jnp.sum(descent_direction * image), ('feed', 'tm'))  38.9 us
    all_to_all x3, blocking collectives, averaged_patch_lines(): lax.all_to_all(slot_parts, 'tm', split_axis=0, concat_axis=0, tiled=True)  37.4 us
    all_to_all x1, blocking collectives, local(): lax.all_to_all(hit_slots, 'tm', split_axis=0, concat_axis=0, tiled=True)  9.73 us
    all_to_all x1, waiting for transfers between devices, averaged_patch_lines(): lax.all_to_all(slot_parts, 'tm', split_axis=0, concat_axis=0, tiled=True)  8.01 us
    dot_general x1, matrix products, local(): jnp.einsum('bsp,bsc->bpc', pix_hot, tod, preferred_element_type=jnp.float32)  7.73 us
  transfers between devices with their start and end apart: 6, of which 4 were waited for; matrix products, arithmetic and copies ran while one was open for 6% of the time, Pallas kernels for 0%

profile of v1, /device:TPU:0, one launch (start us, length us, event | category | flops | bytes accessed | tf_op | source)
XLA Modules:
  0.0 336.7 jit_solution(12535671078461442411)
XLA Ops:
  7.2 1.3 copy.89
  8.5 7.3 %all-to-all-start = ((s32[8,1,1]{2,1,0:T(1,128)}), s32[8,1,1]{2,1,0:T(1,128)S(1)}, u32[]{:S(2)}, u32[]{:S(2)}) async-start(s32[8,1,1]{2,1,0:T(1,128)} %copy.89), calls=%async_computation | async-start | bytes 8192 | tf_op jit(solution)/shard_map/all_to_all | solution.py:34
  15.8 0.9 copy.86
  16.7 7.7 %fusion.54 = (f32[256,256]{1,0:T(8,128)S(1)}, f32[256,32,256]{2,1,0:T(8,128)S(1)}) fusion(bf16[256,50,256]{2,0,1:T(8,128)(2,1)} %param.6, s32[256,50]{1,0:T(8,128)S(1)} %copy.86), kind=kOutput, calls=%fused_computation.82 | convolution fusion | flops 212156416 | bytes 15255552 | tf_op jit(solution)/shard_map/bsp,bsc->bpc/dot_general | solution.py:66
  24.4 0.0 copy-start.3
  24.5 7.7 %fusion = f32[8,32,256]{2,0,1:T(8,128)S(1)} fusion(f32[256,32,256]{2,1,0:T(8,128)S(1)} %get-tuple-element.27, s32[256]{0:T(256)S(1)} %copy-done.1), kind=kOutput, calls=%fused_computation | convolution fusion | flops 201328640 | bytes 8651776 | tf_op jit(solution)/shard_map/bk,bpc->kpc/dot_general | solution.py:67
  32.1 0.8 copy.91
  32.9 0.0 all-to-all-done
  32.9 6.0 %all-to-all-start.1 = ((f32[8,32,256]{2,1,0:T(8,128)}), f32[8,32,256]{2,1,0:T(8,128)S(1)}, u32[]{:S(2)}, u32[]{:S(2)}) async-start(f32[8,32,256]{2,1,0:T(8,128)} %copy.91), calls=%async_computation.1 | async-start | bytes 524288 | tf_op jit(solution)/shard_map/all_to_all | solution.py:45
  38.9 0.0 all-gather.9.cloned.1.call-start
  39.0 0.2 reduce.1
  39.2 0.2 select_reduce_fusion
  39.4 8.0 %all-to-all-done.1 = f32[8,32,256]{2,1,0:T(8,128)S(1)} async-done(((f32[8,32,256]{2,1,0:T(8,128)}), f32[8,32,256]{2,1,0:T(8,128)S(1)}, u32[]{:S(2)}, u32[]{:S(2)}) %all-to-all-start.1) | async-done | bytes 262176 | tf_op jit(solution)/shard_map/all_to_all | solution.py:45
  47.4 1.1 fusion.25
  48.5 0.0 all-gather.9.cloned.1.call-update
  48.6 0.0 all-gather.11.cloned.1.call-start
  48.6 1.2 convert_reduce_fusion
  49.8 0.1 copy.88
  49.9 0.1 multiply_bitcast_fusion
  50.0 9.7 %all_to_all.56 = f32[8,1,32]{2,1,0:T(1,128)S(1)} all-to-all(f32[8,1,32]{2,1,0:T(1,128)S(1)} %bitcast.63), channel_id=1, replica_groups=mesh['feed'=4,'tm'=8] {'tm'}, dimensions={0} | all-to-all | bytes 2048 | tf_op jit(solution)/shard_map/all_to_all | solution.py:33
  59.7 0.2 fusion.49
  59.9 5.6 %psum.35 = f32[8,32]{1,0:T(8,128)S(1)} all-reduce(f32[8,32]{1,0:T(8,128)S(1)} %fusion.49), channel_id=1, replica_groups=mesh['feed'=4,'tm'=8] {'feed'}, use_global_device_ids=true, to_apply=%region_5.6 | all-reduce | flops 256 | bytes 2048 | tf_op jit(solution)/shard_map/psum | solution.py:41
  65.5 0.1 copy.93
  65.6 1.3 bitcast_reduce_fusion.3
  66.9 0.4 fusion.31
  67.3 0.1 copy.95
  67.4 13.4 %all_to_all.57 = f32[8,32,256]{2,1,0:T(8,128)S(1)} all-to-all(f32[8,32,256]{2,1,0:T(8,128)S(1)} %copy.95), channel_id=1, replica_groups=mesh['feed'=4,'tm'=8] {'tm'}, dimensions={0} | all-to-all | bytes 524288 | tf_op jit(solution)/shard_map/all_to_all | solution.py:53
  80.9 0.6 fusion.5
  81.5 0.4 fusion.16
  81.9 12.3 %all_to_all.58 = f32[8,32,256]{2,1,0:T(8,128)S(1)} all-to-all(f32[8,32,256]{2,1,0:T(8,128)S(1)} %fusion.16), channel_id=1, replica_groups=mesh['feed'=4,'tm'=8] {'tm'}, dimensions={0} | all-to-all | bytes 524288 | tf_op jit(solution)/shard_map/all_to_all | solution.py:45
  94.1 1.1 fusion.23
  95.2 0.0 all-gather.11.cloned.1.call-update
  95.3 0.0 all-gather.13.cloned.1.call-start
  95.3 14.9 %all-gather.11.cloned.1.call-done = f32[32,32,256]{2,0,1:T(8,128)} async-done(((f32[8,32,256]{2,0,1:T(8,128)}), f32[32,32,256]{2,0,1:T(8,128)}) %all-gather.11.cloned.1.call-update) | async-done | bytes 1048592 | tf_op jit(solution)/shard_map/all_gather | solution.py:47
  110.2 1.3 bitcast_reduce_fusion.2
  111.5 0.4 fusion.29
  111.9 0.1 copy.98
  112.0 14.6 %all_to_all.59 = f32[8,32,256]{2,1,0:T(8,128)S(1)} all-to-all(f32[8,32,256]{2,1,0:T(8,128)S(1)} %copy.98), channel_id=1, replica_groups=mesh['feed'=4,'tm'=8] {'tm'}, dimensions={0} | all-to-all | bytes 524288 | tf_op jit(solution)/shard_map/all_to_all | solution.py:53
  126.6 1.2 multiply_reduce_fusion.3
  127.8 39.0 %all-reduce = (f32[]{:T(128)}, f32[]{:T(128)}) all-reduce(f32[]{:T(128)} %get-tuple-element.19, f32[]{:T(128)} %get-tuple-element.18), channel_id=1, replica_groups=mesh['feed'=4,'tm'=8] {'feed','tm'}, use_global_device_ids=true, to_apply=%region_7.8 | all-reduce | flops 2 | bytes 16 | tf_op jit(solution)/shard_map/psum | solution.py:63
  168.1 0.7 multiply_reduce_fusion.2
  168.8 40.7 %psum.38 = f32[]{:T(128)} all-reduce(f32[]{:T(128)} %multiply_reduce_fusion.2), channel_id=1, replica_groups=mesh['feed'=4,'tm'=8] {'feed','tm'}, use_global_device_ids=true, to_apply=%region_12.13 | all-reduce | flops 1 | bytes 8 | tf_op jit(solution)/shard_map/psum | solution.py:63
  210.9 0.4 fusion.14
  211.3 12.6 %all_to_all.60 = f32[8,32,256]{2,1,0:T(8,128)S(1)} all-to-all(f32[8,32,256]{2,1,0:T(8,128)S(1)} %fusion.14), channel_id=1, replica_groups=mesh['feed'=4,'tm'=8] {'tm'}, dimensions={0} | all-to-all | bytes 524288 | tf_op jit(solution)/shard_map/all_to_all | solution.py:45
  223.8 1.1 fusion.21
  224.9 0.0 all-gather.13.cloned.1.call-update
  225.0 0.0 all-gather.15.cloned.1.call-start
  225.0 15.0 %all-gather.13.cloned.1.call-done = f32[32,32,256]{2,0,1:T(8,128)} async-done(((f32[8,32,256]{2,0,1:T(8,128)}), f32[32,32,256]{2,0,1:T(8,128)}) %all-gather.13.cloned.1.call-update) | async-done | bytes 1048592 | tf_op jit(solution)/shard_map/all_gather | solution.py:47
  240.0 1.3 bitcast_reduce_fusion.1
  241.3 0.4 fusion.27
  241.7 0.1 copy.101
  241.8 14.6 %all_to_all.61 = f32[8,32,256]{2,1,0:T(8,128)S(1)} all-to-all(f32[8,32,256]{2,1,0:T(8,128)S(1)} %copy.101), channel_id=1, replica_groups=mesh['feed'=4,'tm'=8] {'tm'}, dimensions={0} | all-to-all | bytes 524288 | tf_op jit(solution)/shard_map/all_to_all | solution.py:53
  256.4 1.2 multiply_reduce_fusion.1
  257.6 38.9 %psum.39 = f32[]{:T(128)} all-reduce(f32[]{:T(128)} %get-tuple-element.29), channel_id=1, replica_groups=mesh['feed'=4,'tm'=8] {'feed','tm'}, use_global_device_ids=true, to_apply=%region_15.16 | all-reduce | flops 1 | bytes 8 | tf_op jit(solution)/shard_map/psum | solution.py:79
  297.9 0.8 multiply_subtract_fusion
  298.7 0.5 convolution_subtract_fusion
  299.2 0.1 copy.103
  299.3 12.6 %all_to_all.62 = f32[8,32,256]{2,1,0:T(8,128)S(1)} all-to-all(f32[8,32,256]{2,1,0:T(8,128)S(1)} %copy.103), channel_id=1, replica_groups=mesh['feed'=4,'tm'=8] {'tm'}, dimensions={0} | all-to-all | bytes 524288 | tf_op jit(solution)/shard_map/all_to_all | solution.py:45
  311.8 1.1 fusion.18
  313.0 0.0 all-gather.15.cloned.1.call-update
  313.0 15.0 %all-gather.15.cloned.1.call-done = f32[32,32,256]{2,0,1:T(8,128)} async-done(((f32[8,32,256]{2,0,1:T(8,128)}), f32[32,32,256]{2,0,1:T(8,128)}) %all-gather.15.cloned.1.call-update) | async-done | bytes 1048592 | tf_op jit(solution)/shard_map/all_gather | solution.py:47
  328.0 1.3 bitcast_reduce_fusion
  329.3 0.1 dynamic-slice_multiply_fusion
  329.5 0.7 copy.105
  (13 shorter events, 0.1 us)
Async XLA Ops:
  8.5 24.4 %all-to-all-start = ((s32[8,1,1]{2,1,0:T(1,128)}), s32[8,1,1]{2,1,0:T(1,128)S(1)}, u32[]{:S(2)}, u32[]{:S(2)}) async-start(s32[8,1,1]{2,1,0:T(1,128)} %copy.89), calls=%async_computation | async-start | bytes 8192 | tf_op jit(solution)/shard_map/all_to_all | solution.py:34
  16.7 7.8 %copy-start.1 = (s32[256]{0:T(256)S(1)}, s32[256]{0:T(256)}, u32[]{:S(2)}) copy-start(s32[256]{0:T(256)} %param.8) | copy-start | bytes 3076
  24.4 14.5 %copy-start.3 = (s32[64]{0:T(128)S(1)}, s32[64]{0:T(128)}, u32[]{:S(2)}) copy-start(s32[64]{0:T(128)} %param.10) | copy-start | bytes 772
  32.1 94.5 %copy-start.2 = (f32[256]{0:T(256)S(1)}, f32[256]{0:T(256)}, u32[]{:S(2)}) copy-start(f32[256]{0:T(256)} %param.11) | copy-start | bytes 3076
  32.9 14.5 %all-to-all-start.1 = ((f32[8,32,256]{2,1,0:T(8,128)}), f32[8,32,256]{2,1,0:T(8,128)S(1)}, u32[]{:S(2)}, u32[]{:S(2)}) async-start(f32[8,32,256]{2,1,0:T(8,128)} %copy.91), calls=%async_computation.1 | async-start | bytes 524288 | tf_op jit(solution)/shard_map/all_to_all | solution.py:45
  38.9 26.7 %all-gather.9.cloned.1.call-start = ((), (), s32[]{:S(2)}) async-start(), calls=%async_computation.9 | async-start | bytes 1310720 | tf_op jit(solution)/shard_map/all_gather | solution.py:47
  48.6 61.6 %all-gather.11.cloned.1.call-start = ((), (), s32[]{:S(2)}) async-start(), calls=%async_computation.10 | async-start | bytes 1310720 | tf_op jit(solution)/shard_map/all_gather | solution.py:47
  95.3 144.7 %all-gather.13.cloned.1.call-start = ((), (), s32[]{:S(2)}) async-start(), calls=%async_computation.11 | async-start | bytes 1310720 | tf_op jit(solution)/shard_map/all_gather | solution.py:47
  225.0 103.0 %all-gather.15.cloned.1.call-start = ((), (), s32[]{:S(2)}) async-start(), calls=%async_computation.12 | async-start | bytes 1310720 | tf_op jit(solution)/shard_map/all_gather | solution.py:47
  298.7 31.5 %copy-start = (f32[256,256]{1,0:T(8,128)}, f32[256,256]{1,0:T(8,128)S(1)}, u32[]{:S(2)}) copy-start(f32[256,256]{1,0:T(8,128)S(1)} %get-tuple-element.23) | copy-start | bytes 786436
Sparse Core Ops, SparseCore 0:
  48.7 15.5 all-gather.8
  95.4 14.7 all-gather.10
  225.1 14.8 all-gather.12
  313.1 14.8 all-gather.14
